TPU v7x, 32 devices: a whole 2x2x4 slice. The times are simulated.
32 devices in a mesh: ens: 2 (over y), space: 4 (over z), tm: 2 (over x), mom: 2 (over core).
Axes of the slice: x: 2, y: 2, z: 4, core: 2. Of those that a mesh axis runs over, the one named last changes fastest.
Arguments:
- eigvecs: bfloat16 [8, 2, 3, 256, 2048], P(('ens', 'tm'), None, None, None, 'space'), parts along dimension 0, may hold values from -0.359375 to 0.359375
- momenta: int32 [4, 3], P('mom'), may hold values from 1 to 2
- pairs: int32 [2, 2], replicated, may hold values from 0 to 3, as said below
- spin_weights: float32 [4, 4], replicated, may hold values from -1 to 1
- perambulators: bfloat16 [4, 2, 4, 4, 256, 256], P(('ens', 'tm'), None, None, None, 'space'), parts along dimension 0, may hold values from -0.0234375 to 0.0234375
Outputs:
- blocks: bfloat16 [4, 4, 2, 256, 256], P(('ens', 'tm'), 'mom', None, 'space'), parts along dimension 0
There are 2 independent parts, one for each index of `ens`. A program takes and returns all parts, laid end to end along the dimension named above; an argument that names none is the same for every part. Nothing has to cross between parts.
Inputs may be any that keep to these rules, and one draw needn't show every extreme that they name: pairs[q, 0], the sink, lies in time group q: (q) * 2 <= pairs[q, 0] < (q + 1) * 2; pairs[q, 1], the source, is any timeslice.
All inputs are finite; a program needn't handle non-finite values.
Results may differ from a plain program's by a relative error of at most 0.008.
Values may be sent and summed in bfloat16 or wider, within the bound.
No kernel may reach another device: no remote copies, remote signals or barrier semaphores. Data moves between devices by JAX's collectives and lax.ppermute only.
A program may use at most 64 MiB of HBM per device.

v0:
```python
import math
import jax
import jax.numpy as jnp
from jax import lax
from jax.sharding import PartitionSpec as P

LAT = 48
EXACT_PRECISION = lax.Precision.HIGHEST


def phases(momenta, site_ids):
    xcoord = (site_ids % LAT).astype(jnp.float32)
    ycoord = (site_ids // LAT % LAT).astype(jnp.float32)
    zcoord = (site_ids // (LAT * LAT)).astype(jnp.float32)
    mom_float = momenta.astype(jnp.float32)
    angles = (
        mom_float[:, 0:1] * xcoord + mom_float[:, 1:2] * ycoord + mom_float[:, 2:3] * zcoord
    ) * (2.0 * math.pi / LAT)
    return (jnp.cos(angles), jnp.sin(angles))


def elemental_terms(eigvecs, cosine_rows, sine_rows):
    contract_dims = (((0, 2), (0, 2)), ((), ()))
    per_time = []
    for which_time in range(eigvecs.shape[0]):
        real_vec = eigvecs[which_time, 0]
        imag_vec = eigvecs[which_time, 1]
        real_wide = real_vec.astype(jnp.float32)
        imag_wide = imag_vec.astype(jnp.float32)
        per_mom = []
        for which_mom in range(cosine_rows.shape[0]):
            cosine = cosine_rows[which_mom]
            sine = sine_rows[which_mom]
            real_turned = (cosine * real_wide + sine * imag_wide).astype(jnp.bfloat16)
            imag_turned = (cosine * imag_wide - sine * real_wide).astype(jnp.bfloat16)
            real_part = lax.dot_general(
                real_vec, real_turned, contract_dims, preferred_element_type=jnp.float32
            ) + lax.dot_general(
                imag_vec, imag_turned, contract_dims, preferred_element_type=jnp.float32
            )
            imag_part = lax.dot_general(
                real_vec, imag_turned, contract_dims, preferred_element_type=jnp.float32
            ) - lax.dot_general(
                imag_vec, real_turned, contract_dims, preferred_element_type=jnp.float32
            )
            per_mom.append(jnp.stack([real_part, imag_part]))
        per_time.append(jnp.stack(per_mom))
    return jnp.stack(per_time)


def source_slots(held_rows, pairs, my_group, times_dev, tm_size, pair_dev):
    wanted = pairs[:, 1].reshape(tm_size, pair_dev)
    local_times = jnp.arange(times_dev, dtype=jnp.int32) + my_group * times_dev
    chosen = (wanted[:, :, None] == local_times).astype(jnp.bfloat16)
    return jnp.einsum(
        "rqt,tmcij->rqmcij", chosen, held_rows, preferred_element_type=jnp.float32
    ).astype(jnp.bfloat16)


def sink_select(held_rows, my_pairs, my_group, times_dev):
    local_times = jnp.arange(times_dev, dtype=jnp.int32) + my_group * times_dev
    chosen = (my_pairs[:, 0][:, None] == local_times).astype(jnp.bfloat16)
    return jnp.einsum(
        "qt,tmcij->qmcij", chosen, held_rows, preferred_element_type=jnp.float32
    ).astype(jnp.bfloat16)


def bridge(mixed_block, source):
    real_part = jnp.einsum(
        "qkl,qmjl->qmkj", mixed_block[:, 0], source[:, :, 0], preferred_element_type=jnp.float32
    ) + jnp.einsum(
        "qkl,qmjl->qmkj", mixed_block[:, 1], source[:, :, 1], preferred_element_type=jnp.float32
    )
    imag_part = jnp.einsum(
        "qkl,qmjl->qmkj", mixed_block[:, 1], source[:, :, 0], preferred_element_type=jnp.float32
    ) - jnp.einsum(
        "qkl,qmjl->qmkj", mixed_block[:, 0], source[:, :, 1], preferred_element_type=jnp.float32
    )
    return jnp.stack([real_part, imag_part], 2).astype(jnp.bfloat16)


def attach(sink_elem, bridged):
    real_part = jnp.einsum(
        "qmik,qmkj->qmij", sink_elem[:, :, 0], bridged[:, :, 0], preferred_element_type=jnp.float32
    ) - jnp.einsum(
        "qmik,qmkj->qmij", sink_elem[:, :, 1], bridged[:, :, 1], preferred_element_type=jnp.float32
    )
    imag_part = jnp.einsum(
        "qmik,qmkj->qmij", sink_elem[:, :, 0], bridged[:, :, 1], preferred_element_type=jnp.float32
    ) + jnp.einsum(
        "qmik,qmkj->qmij", sink_elem[:, :, 1], bridged[:, :, 0], preferred_element_type=jnp.float32
    )
    return jnp.stack([real_part, imag_part], 2)


def local(eigvecs, momenta, pairs, spin_weights, perambulators):
    times_dev = eigvecs.shape[0]
    vec_count = eigvecs.shape[3]
    sites_dev = eigvecs.shape[4]
    pair_dev = perambulators.shape[0]
    tm_size = lax.axis_size("tm")
    space_size = lax.axis_size("space")
    my_group = lax.axis_index("tm")
    my_place = lax.axis_index("space")
    rows_dev = vec_count // space_size
    row_first = my_place * rows_dev
    site_ids = my_place * sites_dev + jnp.arange(sites_dev, dtype=jnp.int32)
    cosine_rows, sine_rows = phases(momenta, site_ids)
    partial_value = elemental_terms(eigvecs, cosine_rows, sine_rows)
    my_pairs = lax.dynamic_slice_in_dim(pairs, my_group * pair_dev, pair_dev, 0)
    whole = lax.psum(partial_value, "space").astype(jnp.bfloat16)
    outgoing = source_slots(whole, pairs, my_group, times_dev, tm_size, pair_dev)
    arrived = lax.all_to_all(outgoing, "tm", split_axis=0, concat_axis=0, tiled=True)
    source_full = jnp.sum(arrived, axis=0, dtype=jnp.float32).astype(jnp.bfloat16)
    sink_whole = sink_select(whole, my_pairs, my_group, times_dev)
    sink_own = lax.dynamic_slice_in_dim(sink_whole, row_first, rows_dev, 3)
    mixed_peramb = jnp.einsum(
        "ab,qcabkl->qckl",
        spin_weights,
        perambulators.astype(jnp.float32),
        precision=EXACT_PRECISION,
    ).astype(jnp.bfloat16)
    bridged = bridge(lax.all_gather(mixed_peramb, "space", axis=2, tiled=True), source_full)
    blocks = attach(sink_own, bridged).astype(jnp.bfloat16)
    return blocks


def solution(mesh):
    return jax.shard_map(
        local,
        mesh=mesh,
        in_specs=(
            P(("ens", "tm"), None, None, None, "space"),
            P("mom", None),
            P(),
            P(),
            P(("ens", "tm"), None, None, None, "space", None),
        ),
        out_specs=P(("ens", "tm"), "mom", None, "space", None),
        check_vma=False,
    )
```

profile of v0, /device:TPU:0, one launch (start us, length us, event | category | flops | bytes accessed | tf_op | source)
XLA Modules:
  0.0 120.1 jit_solution(8111220607492806430)
XLA Ops:
  0.0 0.8 convert_element_type.166
  1.3 2.2 %convolution_bitcast_fusion.14 = f32[256,256]{1,0:T(8,128)S(1)} fusion(f32[512]{0:T(512)S(1)} %bitcast.288, f32[512]{0:T(512)S(1)} %bitcast.296, bf16[2,2,3,256,512]{4,3,2,1,0:T(8,128)(2,1)} %param.5), kind=kOutput, calls=%fused_computation.55 | convolution fusion | flops 203685888 | bytes 2625536 | tf_op jit(solution)/shard_map/dot_general | solution.py:38
  3.5 0.4 copy-done.1
  3.9 0.4 convolution_bitcast_fusion.12
  4.3 0.5 convolution_bitcast_fusion.10
  4.8 0.4 convolution_bitcast_fusion.8
  5.2 0.4 convolution_bitcast_fusion.6
  5.7 0.5 convolution_bitcast_fusion.4
  6.1 0.5 convolution_bitcast_fusion.2
  6.6 0.4 convolution_bitcast_fusion
  7.1 0.4 fusion.22
  7.5 0.5 fusion.24
  8.0 0.5 fusion.26
  8.4 0.5 fusion.28
  8.9 0.5 fusion.30
  9.4 0.5 fusion.32
  9.8 0.5 fusion.34
  10.3 0.5 fusion.36
  11.2 79.3 %all-reduce.1 = bf16[2,2,2,256,256]{3,4,2,1,0:T(8,128)(2,1)} all-reduce(f32[2,2,2,256,256]{3,4,2,1,0:T(8,128)S(1)} %pad_maximum_fusion), channel_id=1, replica_groups=mesh['ens'=2,'space'=4,'tm'=2,'mom'=2] {'space'}, use_global_device_ids=true, to_apply=%region_0.1 | all-reduce | flops 524288 | bytes 3145728 | tf_op jit(solution)/shard_map/psum | solution.py:111
  90.5 2.5 %copy.12 = bf16[2,2,2,256,256]{4,0,3,2,1:T(2,128)(2,1)S(1)} copy(bf16[2,2,2,256,256]{3,4,2,1,0:T(8,128)(2,1)} %all-reduce.1) | data formatting | bytes 2097152 | tf_op jit(solution)/shard_map/convert_element_type | solution.py:111
  93.3 1.3 %fusion.16 = bf16[2,1,2,2,256,256]{5,0,4,3,2,1:T(2,128)(2,1)S(1)} fusion(bf16[2,2,2,256,256]{4,0,3,2,1:T(2,128)(2,1)S(1)} %copy.12, s32[2]{0:T(128)S(1)} %iota_add_fusion.1, s32[2]{0:T(128)S(1)} %slice_reduce_fusion), kind=kOutput, calls=%fused_computation.34 | convolution fusion | flops 2621444 | bytes 2097168 | tf_op jit(solution)/shard_map/rqt,tmcij->rqmcij/dot_general | solution.py:55
  94.6 1.1 copy.13
  95.7 3.9 %all-to-all-start = ((bf16[2,1,2,2,256,256]{5,4,3,2,1,0:T(8,128)(2,1)}), bf16[2,1,2,2,256,256]{5,4,3,2,1,0:T(8,128)(2,1)S(1)}, u32[]{:S(2)}, u32[]{:S(2)}) async-start(bf16[2,1,2,2,256,256]{5,4,3,2,1,0:T(8,128)(2,1)} %copy.13), calls=%async_computation | async-start | bytes 2097152 | tf_op jit(solution)/shard_map/all_to_all | solution.py:113
  99.6 2.1 %fusion.41 = bf16[1,2,64,256,1]{3,0,4,2,1:T(2,128)(2,1)S(1)} fusion(f32[4,4,1,1,1]{1,2,0,4,3:T(1,128)S(1)} %bitcast.304, bf16[2,4,4,64,256]{4,3,2,1,0:T(8,128)(2,1)S(1)} %bitcast.261), kind=kOutput, calls=%fused_computation.82 | convolution fusion | flops 6291456 | bytes 1114176 | tf_op jit(solution)/shard_map/ab,qcabkl->qckl/dot_general | solution.py:117
  101.8 1.3 %fusion.145 = bf16[1,2,2,256,256]{4,0,3,2,1:T(2,128)(2,1)S(1)} fusion(bf16[2,2,2,256,256]{4,0,3,2,1:T(2,128)(2,1)S(1)} %copy.12, s32[]{:T(128)S(1)} %bitcast.305, s32[]{:T(128)S(6)} %mul.205), kind=kOutput, calls=%fused_computation.194 | convolution fusion | flops 1048580 | bytes 1572872 | tf_op jit(solution)/shard_map/qt,tmcij->qmcij/dot_general | solution.py:63
  103.1 13.8 %all-gather = bf16[2,256,256]{2,1,0:T(8,128)(2,1)S(1)} all-gather(bf16[2,64,256]{2,1,0:T(8,128)(2,1)S(1)} %bitcast.271), channel_id=2, replica_groups=mesh['ens'=2,'space'=4,'tm'=2,'mom'=2] {'space'}, dimensions={1}, use_global_device_ids=true | all-gather | bytes 327680 | tf_op jit(solution)/shard_map/all_gather | solution.py:123
  116.9 0.5 reduce_sum.14
  117.5 0.2 fusion.100
  117.7 0.3 fusion.99
  118.0 0.3 fusion.20
  118.3 0.3 fusion.19
  119.4 0.7 copy.20
  (34 shorter events, 2.1 us)
Async XLA Ops:
  0.0 99.6 %copy-start = (bf16[1,2,4,4,64,256]{5,4,3,2,1,0:T(8,128)(2,1)S(1)}, bf16[1,2,4,4,64,256]{5,4,3,2,1,0:T(8,128)(2,1)}, u32[]{:S(2)}) copy-start(bf16[1,2,4,4,64,256]{5,4,3,2,1,0:T(8,128)(2,1)} %param.9) | copy-start | bytes 3145732
  1.3 2.6 %copy-start.1 = (bf16[2,2,3,256,512]{4,3,2,1,0:T(8,128)(2,1)S(1)}, bf16[2,2,3,256,512]{4,3,2,1,0:T(8,128)(2,1)}, u32[]{:S(2)}) copy-start(bf16[2,2,3,256,512]{4,3,2,1,0:T(8,128)(2,1)} %param.5) | copy-start | bytes 9437188
  90.5 2.6 %copy-start.3 = (s32[2,2]{1,0:T(2,128)S(1)}, s32[2,2]{1,0:T(2,128)}, u32[]{:S(2)}) copy-start(s32[2,2]{1,0:T(2,128)} %param.7) | copy-start | bytes 52
  95.7 3.9 %copy-start.2 = (f32[4,4]{1,0:T(4,128)S(1)}, f32[4,4]{1,0:T(4,128)}, u32[]{:S(2)}) copy-start(f32[4,4]{1,0:T(4,128)} %param.8) | copy-start | bytes 196
  95.7 21.2 %all-to-all-start = ((bf16[2,1,2,2,256,256]{5,4,3,2,1,0:T(8,128)(2,1)}), bf16[2,1,2,2,256,256]{5,4,3,2,1,0:T(8,128)(2,1)S(1)}, u32[]{:S(2)}, u32[]{:S(2)}) async-start(bf16[2,1,2,2,256,256]{5,4,3,2,1,0:T(8,128)(2,1)} %copy.13), calls=%async_computation | async-start | bytes 2097152 | tf_op jit(solution)/shard_map/all_to_all | solution.py:113
where the time goes:
time: 120 us
  blocking collectives  93.1 us (78%)
  matrix products  15.5 us (13%)
  local copies, waits for them, and re-layouts  5.32 us (4%)
  starting transfers between devices  3.89 us (3%)
  other arithmetic  1.86 us (2%)
    psum x1, blocking collectives, local(): whole = lax.psum(partial_value, 'space').astype(jnp.bfloat16)  79.3 us
    all_gather x1, blocking collectives, local(): lax.all_gather(mixed_peramb, 'space', axis=2, tiled=True)  13.8 us
    all_to_all x1, starting transfers between devices, local(): lax.all_to_all(outgoing, 'tm', split_axis=0, concat_axis=0, tiled=True)  3.89 us
    dot_general x4, matrix products, elemental_terms(): lax.dot_general(imag_vec, imag_turned, contract_dims, preferred_element_t...  3.57 us
    convert_element_type x1, local copies, waits for them, and re-layouts, local(): whole = lax.psum(partial_value, 'space').astype(jnp.bfloat16)  2.54 us
  transfers between devices with their start and end apart: 1, of which 0 were waited for; matrix products, arithmetic and copies ran while one was open for 3% of the time, Pallas kernels for 0%

commit v1 on v0

--- a/solution.py
+++ b/solution.py
@@ -6,6 +6,14 @@
 
 LAT = 48
 EXACT_PRECISION = lax.Precision.HIGHEST
+
+
+def gather_from_all(array, axis, dim):
+    peers = lax.axis_size(axis)
+    repeats = [peers if d == dim else 1 for d in range(array.ndim)]
+    return lax.all_to_all(
+        jnp.tile(array, repeats), axis, split_axis=dim, concat_axis=dim, tiled=True
+    )
 
 
 def phases(momenta, site_ids):
@@ -120,7 +128,7 @@
         perambulators.astype(jnp.float32),
         precision=EXACT_PRECISION,
     ).astype(jnp.bfloat16)
-    bridged = bridge(lax.all_gather(mixed_peramb, "space", axis=2, tiled=True), source_full)
+    bridged = bridge(gather_from_all(mixed_peramb, "space", 2), source_full)
     blocks = attach(sink_own, bridged).astype(jnp.bfloat16)
     return blocks
 

time: 120 us -> 121 us (level)
  blocking collectives: 93.1 us -> 77 us
  waiting for transfers between devices: 0.01 us -> 8.18 us
  starting transfers between devices: 3.89 us -> 9.94 us
  local copies, waits for them, and re-layouts: 5.32 us -> 7.86 us
    all_gather x1 -> x0, blocking collectives: 13.8 us -> none  [local(): lax.all_gather(mixed_peramb, 'space', axis=2, tiled=True)]
    all_to_all x1, waiting for transfers between devices: 0.01 us -> 8.17 us  [local(): lax.all_to_all(outgoing, 'tm', split_axis=0, concat_axis=0, tiled=True)]
    all_to_all x0 -> x1, starting transfers between devices: none -> 6.35 us  [gather_from_all(): lax.all_to_all(jnp.tile(array, repeats), axis, split_axis=dim, concat_axi...]
    psum x1, blocking collectives: 79.3 us -> 77 us  [local(): whole = lax.psum(partial_value, 'space').astype(jnp.bfloat16)]
    unnamed x8, local copies, waits for them, and re-layouts: 0.38 us -> 1.6 us
  transfers between devices with their start and end apart: 1 -> 2, of which waited for: 0 -> 1; matrix products, arithmetic and copies ran while one was open for 3% -> 14% of each run, Pallas kernels for 0% -> 0%
where the time goes in v1:
time: 121 us
  blocking collectives  77 us (64%)
  matrix products  16.2 us (13%)
  starting transfers between devices  9.94 us (8%)
  waiting for transfers between devices  8.18 us (7%)
  local copies, waits for them, and re-layouts  7.86 us (6%)
    psum x1, blocking collectives, local(): whole = lax.psum(partial_value, 'space').astype(jnp.bfloat16)  77 us
    all_to_all x1, waiting for transfers between devices, local(): lax.all_to_all(outgoing, 'tm', split_axis=0, concat_axis=0, tiled=True)  8.17 us
    all_to_all x1, starting transfers between devices, gather_from_all(): lax.all_to_all(jnp.tile(array, repeats), axis, split_axis=dim, concat_axi...  6.35 us
    all_to_all x1, starting transfers between devices, local(): lax.all_to_all(outgoing, 'tm', split_axis=0, concat_axis=0, tiled=True)  3.59 us
    dot_general x4, matrix products, elemental_terms(): lax.dot_general(imag_vec, imag_turned, contract_dims, preferred_element_t...  3.57 us
    dot_general x1, matrix products, local(): jnp.einsum('ab,qcabkl->qckl', spin_weights, perambulators.astype(jnp.floa...  2.8 us
    convert_element_type x1, local copies, waits for them, and re-layouts, local(): whole = lax.psum(partial_value, 'space').astype(jnp.bfloat16)  2.54 us
  transfers between devices with their start and end apart: 2, of which 1 were waited for; matrix products, arithmetic and copies ran while one was open for 14% of the time, Pallas kernels for 0%

profile of v1, /device:TPU:0, one launch (start us, length us, event | category | flops | bytes accessed | tf_op | source)
XLA Modules:
  0.0 120.7 jit_solution(16919143586066798621)
XLA Ops:
  0.0 1.2 %copy-done = bf16[1,2,4,4,64,256]{5,4,3,2,1,0:T(8,128)(2,1)S(1)} copy-done((bf16[1,2,4,4,64,256]{5,4,3,2,1,0:T(8,128)(2,1)S(1)}, bf16[1,2,4,4,64,256]{5,4,3,2,1,0:T(8,128)(2,1)}, u32[]{:S(2)}) %copy-start) | copy-done | bytes 1048600
  1.2 2.8 %fusion.41 = bf16[1,2,64,256,1]{3,0,4,2,1:T(2,128)(2,1)S(1)} fusion(f32[4,4,1,1,1]{1,2,0,4,3:T(1,128)} %bitcast.300, bf16[2,4,4,64,256]{4,3,2,1,0:T(8,128)(2,1)S(1)} %bitcast.261), kind=kOutput, calls=%fused_computation.82 | convolution fusion | flops 6291456 | bytes 1114176 | tf_op jit(solution)/shard_map/ab,qcabkl->qckl/dot_general | solution.py:125
  4.1 0.9 tile.4
  5.0 6.3 %all-to-all-start.1 = ((bf16[1,2,256,256]{3,1,0,2:T(2,128)(2,1)}), bf16[1,2,256,256]{3,1,0,2:T(2,128)(2,1)S(1)}, u32[]{:S(2)}, u32[]{:S(2)}) async-start(bf16[1,2,256,256]{3,1,0,2:T(2,128)(2,1)} %bitcast.69), calls=%async_computation.1 | async-start | bytes 524288 | tf_op jit(solution)/shard_map/all_to_all | solution.py:14
  11.9 2.2 %convolution_bitcast_fusion.14 = f32[256,256]{1,0:T(8,128)S(1)} fusion(f32[512]{0:T(512)S(1)} %bitcast.284, f32[512]{0:T(512)S(1)} %bitcast.292, bf16[2,2,3,256,512]{4,3,2,1,0:T(8,128)(2,1)} %param.5), kind=kOutput, calls=%fused_computation.55 | convolution fusion | flops 203685888 | bytes 2625536 | tf_op jit(solution)/shard_map/dot_general | solution.py:46
  14.1 0.4 copy-done.2
  14.5 0.4 convolution_bitcast_fusion.12
  14.9 0.5 convolution_bitcast_fusion.10
  15.4 0.4 convolution_bitcast_fusion.8
  15.8 0.5 convolution_bitcast_fusion.6
  16.3 0.5 convolution_bitcast_fusion.4
  16.7 0.5 convolution_bitcast_fusion.2
  17.2 0.4 convolution_bitcast_fusion
  17.7 0.4 fusion.22
  18.1 0.5 fusion.24
  18.6 0.5 fusion.26
  19.0 0.5 fusion.28
  19.5 0.5 fusion.30
  20.0 0.5 fusion.32
  20.4 0.5 fusion.34
  20.9 0.5 fusion.36
  21.8 77.0 %all-reduce.1 = bf16[2,2,2,256,256]{3,4,2,1,0:T(8,128)(2,1)} all-reduce(f32[2,2,2,256,256]{3,4,2,1,0:T(8,128)S(1)} %pad_maximum_fusion), channel_id=1, replica_groups=mesh['ens'=2,'space'=4,'tm'=2,'mom'=2] {'space'}, use_global_device_ids=true, to_apply=%region_0.1 | all-reduce | flops 524288 | bytes 3145728 | tf_op jit(solution)/shard_map/psum | solution.py:119
  99.0 2.5 %copy.12 = bf16[2,2,2,256,256]{4,0,3,2,1:T(2,128)(2,1)S(1)} copy(bf16[2,2,2,256,256]{3,4,2,1,0:T(8,128)(2,1)} %all-reduce.1) | data formatting | bytes 2097152 | tf_op jit(solution)/shard_map/convert_element_type | solution.py:119
  101.6 1.3 %fusion.16 = bf16[2,1,2,2,256,256]{5,0,4,3,2,1:T(2,128)(2,1)S(1)} fusion(bf16[2,2,2,256,256]{4,0,3,2,1:T(2,128)(2,1)S(1)} %copy.12, s32[2]{0:T(128)S(1)} %iota_add_fusion.1, s32[2]{0:T(128)S(1)} %slice_reduce_fusion), kind=kOutput, calls=%fused_computation.34 | convolution fusion | flops 2621444 | bytes 2097168 | tf_op jit(solution)/shard_map/rqt,tmcij->rqmcij/dot_general | solution.py:63
  102.9 1.1 copy.13
  104.0 3.6 %all-to-all-start = ((bf16[2,1,2,2,256,256]{5,4,3,2,1,0:T(8,128)(2,1)}), bf16[2,1,2,2,256,256]{5,4,3,2,1,0:T(8,128)(2,1)S(1)}, u32[]{:S(2)}, u32[]{:S(2)}) async-start(bf16[2,1,2,2,256,256]{5,4,3,2,1,0:T(8,128)(2,1)} %copy.13), calls=%async_computation | async-start | bytes 2097152 | tf_op jit(solution)/shard_map/all_to_all | solution.py:121
  107.6 1.3 %fusion.145 = bf16[1,2,2,256,256]{4,0,3,2,1:T(2,128)(2,1)S(1)} fusion(bf16[2,2,2,256,256]{4,0,3,2,1:T(2,128)(2,1)S(1)} %copy.12, s32[]{:T(128)S(1)} %bitcast.301, s32[]{:T(128)S(6)} %mul.205), kind=kOutput, calls=%fused_computation.194 | convolution fusion | flops 1048580 | bytes 1572872 | tf_op jit(solution)/shard_map/qt,tmcij->qmcij/dot_general | solution.py:71
  109.0 0.4 fusion.150
  109.4 8.2 %all-to-all-done = bf16[2,1,2,2,256,256]{5,4,3,2,1,0:T(8,128)(2,1)S(1)} async-done(((bf16[2,1,2,2,256,256]{5,4,3,2,1,0:T(8,128)(2,1)}), bf16[2,1,2,2,256,256]{5,4,3,2,1,0:T(8,128)(2,1)S(1)}, u32[]{:S(2)}, u32[]{:S(2)}) %all-to-all-start) | async-done | bytes 1048608 | tf_op jit(solution)/shard_map/all_to_all | solution.py:121
  117.6 0.5 reduce_sum.14
  118.9 0.3 fusion.19
  120.0 0.7 copy.22
  (37 shorter events, 3.0 us)
Async XLA Ops:
  0.0 1.2 %copy-start = (bf16[1,2,4,4,64,256]{5,4,3,2,1,0:T(8,128)(2,1)S(1)}, bf16[1,2,4,4,64,256]{5,4,3,2,1,0:T(8,128)(2,1)}, u32[]{:S(2)}) copy-start(bf16[1,2,4,4,64,256]{5,4,3,2,1,0:T(8,128)(2,1)} %param.9) | copy-start | bytes 3145732
  1.2 10.2 %copy-start.1 = (s32[2,3]{1,0:T(2,128)S(1)}, s32[2,3]{1,0:T(2,128)}, u32[]{:S(2)}) copy-start(s32[2,3]{1,0:T(2,128)} %param.6) | copy-start | bytes 76
  5.0 99.0 %all-to-all-start.1 = ((bf16[1,2,256,256]{3,1,0,2:T(2,128)(2,1)}), bf16[1,2,256,256]{3,1,0,2:T(2,128)(2,1)S(1)}, u32[]{:S(2)}, u32[]{:S(2)}) async-start(bf16[1,2,256,256]{3,1,0,2:T(2,128)(2,1)} %bitcast.69), calls=%async_computation.1 | async-start | bytes 524288 | tf_op jit(solution)/shard_map/all_to_all | solution.py:14
  11.9 2.6 %copy-start.2 = (bf16[2,2,3,256,512]{4,3,2,1,0:T(8,128)(2,1)S(1)}, bf16[2,2,3,256,512]{4,3,2,1,0:T(8,128)(2,1)}, u32[]{:S(2)}) copy-start(bf16[2,2,3,256,512]{4,3,2,1,0:T(8,128)(2,1)} %param.5) | copy-start | bytes 9437188
  21.8 77.0 %copy-start.3 = (s32[2,2]{1,0:T(2,128)S(1)}, s32[2,2]{1,0:T(2,128)}, u32[]{:S(2)}) copy-start(s32[2,2]{1,0:T(2,128)} %param.7) | copy-start | bytes 52
  104.0 13.5 %all-to-all-start = ((bf16[2,1,2,2,256,256]{5,4,3,2,1,0:T(8,128)(2,1)}), bf16[2,1,2,2,256,256]{5,4,3,2,1,0:T(8,128)(2,1)S(1)}, u32[]{:S(2)}, u32[]{:S(2)}) async-start(bf16[2,1,2,2,256,256]{5,4,3,2,1,0:T(8,128)(2,1)} %copy.13), calls=%async_computation | async-start | bytes 2097152 | tf_op jit(solution)/shard_map/all_to_all | solution.py:121
